TPU v7x, 256 devices: a whole 4x4x8 slice. The times are simulated.
256 devices in a mesh: aux: 2 (over core), row: 8 (over z), col: 16 (over x, y).
Axes of the slice: x: 4, y: 4, z: 8, core: 2. Of those that a mesh axis runs over, the one named last changes fastest.
Arguments:
- coulomb: bfloat16 [64, 2048, 2048], P('aux', 'row', 'col'), may hold values from -6 to 6
- occupied: bfloat16 [2048, 2048], P('row'), may hold values from -0.125 to 0.125
- virtual: bfloat16 [2048, 2048], P('row'), may hold values from -0.125 to 0.125
- tile_mask: int32 [16, 16], replicated, may hold values 0 or 1
Outputs:
- chi: float32 [64, 64], P('aux')
All inputs are finite; a program needn't handle non-finite values.
Results may differ from a plain program's by a relative error of at most 0.0042.
Values may be sent and summed in bfloat16 or wider, within the bound.
A program may use at most 128 MiB of HBM per device.

v0:
```python
import jax
import jax.numpy as jnp
from jax import lax
from jax.sharding import PartitionSpec as P

NAO = 2048
TILE = 128


def swapped(value, axis, apart):
    mask = 2**apart
    pairs = [(source, source ^ mask) for source in range(lax.axis_size(axis))]
    return lax.ppermute(value, axis, pairs)


def shards(coulomb, occupied, virtual, tile_mask):
    rows = lax.axis_size("row")
    cols = lax.axis_size("col")
    pdev, mrow, ncol = coulomb.shape
    nao = mrow * rows
    row_idx = lax.axis_index("row")
    col_idx = lax.axis_index("col")
    aux_idx = lax.axis_index("aux")
    tiles_r = mrow // TILE
    tiles_c = ncol // TILE
    local_tiles = lax.dynamic_slice(
        tile_mask, (row_idx * tiles_r, col_idx * tiles_c), (tiles_r, tiles_c)
    )
    local_mask = jnp.repeat(jnp.repeat(local_tiles, TILE, axis=0), TILE, axis=1).astype(
        jnp.bfloat16
    )
    screened = coulomb * local_mask[None]
    moved = lax.all_to_all(screened, "row", split_axis=0, concat_axis=1, tiled=True)
    pieces = moved.shape[0]
    occ_all, virt_all = (
        lax.all_gather(occupied, "row", axis=0, tiled=True),
        lax.all_gather(virtual, "row", axis=0, tiled=True),
    )
    half = jnp.einsum("ml,pmn->pln", occ_all, moved, preferred_element_type=jnp.float32).astype(
        jnp.bfloat16
    )
    jpart = mrow // cols
    shaped = half.reshape(pieces, rows, cols, jpart, ncol)
    spread = lax.all_to_all(shaped, "col", split_axis=2, concat_axis=4, tiled=True)
    spread = spread.reshape(pieces, rows * jpart, nao)
    dressed = jnp.einsum(
        "pln,ns->pls", spread, virt_all, preferred_element_type=jnp.float32
    ).astype(jnp.bfloat16)
    layered = dressed.reshape(pieces, rows, 1, jpart, cols, ncol)
    returned = lax.all_to_all(
        lax.all_to_all(layered, "row", split_axis=1, concat_axis=0, tiled=True),
        "col",
        split_axis=4,
        concat_axis=2,
        tiled=True,
    )
    aligned = returned.reshape(pdev, mrow, ncol)
    theirs = swapped(screened, "aux", 0)
    with_mine = jnp.einsum("pls,qls->pq", aligned, screened, preferred_element_type=jnp.float32)
    with_theirs = jnp.einsum("pls,qls->pq", aligned, theirs, preferred_element_type=jnp.float32)
    first_half = jnp.where(aux_idx == 0, with_mine, with_theirs)
    second_half = jnp.where(aux_idx == 0, with_theirs, with_mine)
    partial_chi = jnp.concatenate([first_half, second_half], axis=1)
    total_chi = lax.psum(partial_chi, ("row", "col"))
    return total_chi / NAO


def solution(mesh):
    placed = (P("aux", "row", "col"), P("row", None), P("row", None), P())
    return jax.shard_map(
        shards, mesh=mesh, in_specs=placed, out_specs=P("aux", None), check_vma=False
    )
```

profile of v0, /device:TPU:0, one launch (start us, length us, event | category | flops | bytes accessed | tf_op | source)
XLA Modules:
  0.0 1038.5 jit_solution(6755601709993652313)
XLA Ops:
  6.5 0.0 all-gather.3.cloned.1.call-start
  6.5 0.7 all-gather.3.cloned.1.call-update
  7.3 0.0 all-gather.5.cloned.1.call-start
  7.3 0.7 all-gather.5.cloned.1.call-update
  8.0 0.9 fusion.13
  8.9 0.1 broadcast_bitcast_fusion
  9.0 2.8 copy_multiply_fusion
  11.7 0.8 copy.15
  12.6 80.1 %all_to_all.66 = bf16[32,256,128]{2,1,0:T(8,128)(2,1)} all-to-all(bf16[32,256,128]{2,1,0:T(8,128)(2,1)S(1)} %copy.15), channel_id=1, replica_groups=mesh['aux'=2,'row'=8,'col'=16] {'row'}, dimensions={0} | all-to-all | bytes 4194304 | tf_op jit(solution)/shard_map/all_to_all | solution.py:33
  92.7 4.5 copy.16
  97.2 4.2 all_to_all.51
  101.4 45.5 %all-gather.3.cloned.1.call-done = bf16[2048,2048]{1,0:T(8,128)(2,1)} async-done(((bf16[256,2048]{1,0:T(8,128)(2,1)}), bf16[2048,2048]{1,0:T(8,128)(2,1)}) %all-gather.3.cloned.1.call-update) | async-done | bytes 8388624 | tf_op jit(solution)/shard_map/all_gather | solution.py:36
  146.9 9.8 fusion.10
  156.7 3.9 copy.17
  160.6 2.2 copy.18
  162.8 35.3 %all_to_all.67 = bf16[4,8,16,16,128]{4,3,1,0,2:T(8,128)(2,1)S(1)} all-to-all(bf16[4,8,16,16,128]{4,3,1,0,2:T(8,128)(2,1)S(1)} %copy.18), channel_id=1, replica_groups=mesh['aux'=2,'row'=8,'col'=16] {'col'}, dimensions={2} | all-to-all | bytes 4194304 | tf_op jit(solution)/shard_map/all_to_all | solution.py:44
  198.1 3.7 copy.19
  201.9 4.2 reshape.35
  206.0 35.8 %all-gather.5.cloned.1.call-done = bf16[2048,2048]{1,0:T(8,128)(2,1)} async-done(((bf16[256,2048]{1,0:T(8,128)(2,1)}), bf16[2048,2048]{1,0:T(8,128)(2,1)}) %all-gather.5.cloned.1.call-update) | async-done | bytes 8388624 | tf_op jit(solution)/shard_map/all_gather | solution.py:37
  241.9 8.5 fusion.7
  250.4 0.6 copy.23
  251.0 0.6 copy.20
  251.6 55.3 %all_to_all.68 = bf16[4,8,1,16,16,128]{5,4,3,0,2,1:T(8,128)(2,1)S(1)} all-to-all(bf16[4,8,1,16,16,128]{5,4,3,0,2,1:T(8,128)(2,1)S(1)} %copy.20), channel_id=1, replica_groups=mesh['aux'=2,'row'=8,'col'=16] {'row'}, dimensions={1} | all-to-all | bytes 4194304 | tf_op jit(solution)/shard_map/all_to_all | solution.py:51
  306.9 1.8 copy.21
  308.8 6.9 all-to-all-start.3
  315.6 0.1 collective-permute-start
  315.7 27.9 %all-to-all-done.3 = bf16[32,1,1,16,16,128]{5,3,0,2,1,4:T(8,128)(2,1)} async-done(((bf16[32,1,1,16,16,128]{5,3,0,2,1,4:T(8,128)(2,1)}), bf16[32,1,1,16,16,128]{5,3,0,2,1,4:T(8,128)(2,1)}, u32[]{:S(2)}, u32[]{:S(2)}) %all-to-all-start.3) | async-done | bytes 2097184 | tf_op jit(solution)/shard_map/all_to_all | solution.py:50
  343.7 2.1 copy.22
  345.8 0.7 convolution_bitcast_fusion.1
  346.5 0.0 collective-permute-done
  346.5 2.3 broadcast_select_fusion.1
  348.8 0.1 pad_maximum_fusion
  348.9 682.2 %psum.7 = f32[32,64]{1,0:T(8,128)S(1)} all-reduce(f32[32,64]{1,0:T(8,128)S(1)} %pad_maximum_fusion), channel_id=1, replica_groups=mesh['aux'=2,'row'=8,'col'=16] {'row','col'}, use_global_device_ids=true, to_apply=%region_0.1 | all-reduce | flops 2048 | bytes 16384 | tf_op jit(solution)/shard_map/psum | solution.py:64
  1031.1 0.6 broadcast_multiply_fusion
Async XLA Ops:
  6.5 140.3 %all-gather.3.cloned.1.call-start = ((), (), s32[]{:S(2)}) async-start(), calls=%async_computation.4 | async-start | bytes 9437184 | tf_op jit(solution)/shard_map/all_gather | solution.py:36
  7.3 234.6 %all-gather.5.cloned.1.call-start = ((), (), s32[]{:S(2)}) async-start(), calls=%async_computation.5 | async-start | bytes 9437184 | tf_op jit(solution)/shard_map/all_gather | solution.py:37
  308.8 34.9 %all-to-all-start.3 = ((bf16[32,1,1,16,16,128]{5,3,0,2,1,4:T(8,128)(2,1)}), bf16[32,1,1,16,16,128]{5,3,0,2,1,4:T(8,128)(2,1)}, u32[]{:S(2)}, u32[]{:S(2)}) async-start(bf16[32,1,1,16,16,128]{5,3,0,2,1,4:T(8,128)(2,1)} %copy.21), calls=%async_computation.3 | async-start | bytes 4194304 | tf_op jit(solution)/shard_map/all_to_all | solution.py:50
  315.6 30.8 %collective-permute-start = (bf16[32,256,128]{2,0,1:T(8,128)(2,1)S(1)}, bf16[32,256,128]{2,0,1:T(8,128)(2,1)}, u32[]{:S(2)}, u32[]{:S(2)}) collective-permute-start(bf16[32,256,128]{2,0,1:T(8,128)(2,1)S(1)} %copy_multiply_fusion), channel_id=1, source_target_pairs={{0,128},{128,0},{1,129},{129,1},{2,130},{130,2},{3,131},{131,3},{4... | collective-permute-start | bytes 6291464 | tf_op jit(solution)/shard_map/ppermute | solution.py:13
Sparse Core Ops, SparseCore 0:
  9.1 137.6 all-gather.2
  148.7 93.1 all-gather.4
where the time goes:
time: 1040 us
  blocking collectives  853 us (82%)
  waiting for transfers between devices  111 us (11%)
  local copies, waits for them, and re-layouts  28.8 us (3%)
  matrix products  21.3 us (2%)
  between operations  13.5 us (1%)
    psum x1, blocking collectives, shards(): total_chi = lax.psum(partial_chi, ('row', 'col'))  682 us
    all_to_all x1, blocking collectives, shards(): lax.all_to_all(screened, 'row', split_axis=0, concat_axis=1, tiled=True)  80.1 us
    all_to_all x1, blocking collectives, shards(): lax.all_to_all(layered, 'row', split_axis=1, concat_axis=0, tiled=True)  55.3 us
    all_gather x1, waiting for transfers between devices, shards(): lax.all_gather(occupied, 'row', axis=0, tiled=True)  45.5 us
    all_gather x1, waiting for transfers between devices, shards(): lax.all_gather(virtual, 'row', axis=0, tiled=True)  35.8 us
    all_to_all x1, blocking collectives, shards(): lax.all_to_all(shaped, 'col', split_axis=2, concat_axis=4, tiled=True)  35.3 us
    all_to_all x1, waiting for transfers between devices, shards(): lax.all_to_all(lax.all_to_all(layered, 'row', split_axis=1, concat_axis=0...  27.9 us
  transfers between devices with their start and end apart: 4, of which 3 were waited for; matrix products, arithmetic and copies ran while one was open for 3% of the time, Pallas kernels for 0%

commit v1 on v0

--- a/solution.py
+++ b/solution.py
@@ -61,7 +61,7 @@
     first_half = jnp.where(aux_idx == 0, with_mine, with_theirs)
     second_half = jnp.where(aux_idx == 0, with_theirs, with_mine)
     partial_chi = jnp.concatenate([first_half, second_half], axis=1)
-    total_chi = lax.psum(partial_chi, ("row", "col"))
+    total_chi = lax.psum(lax.psum(partial_chi, axis_name="col"), axis_name="row")
     return total_chi / NAO
 
 

time: 1040 us -> 455 us (0.44)
  blocking collectives: 853 us -> 269 us
    psum x1 -> x2, blocking collectives: 682 us -> 98.3 us  [the longest x1 70.5 us: shards(): lax.psum(partial_chi, axis_name='col')]
  transfers between devices with their start and end apart: 4 -> 4, of which waited for: 3 -> 3; matrix products, arithmetic and copies ran while one was open for 3% -> 8% of each run, Pallas kernels for 0% -> 0%
where the time goes in v1:
time: 455 us
  blocking collectives  269 us (59%)
  waiting for transfers between devices  111 us (24%)
  local copies, waits for them, and re-layouts  28.8 us (6%)
  matrix products  21.3 us (5%)
  between operations  13.5 us (3%)
  starting transfers between devices  6.99 us (2%)
    all_to_all x1, blocking collectives, shards(): lax.all_to_all(screened, 'row', split_axis=0, concat_axis=1, tiled=True)  80.1 us
    psum x1, blocking collectives, shards(): lax.psum(partial_chi, axis_name='col')  70.5 us
    all_to_all x1, blocking collectives, shards(): lax.all_to_all(layered, 'row', split_axis=1, concat_axis=0, tiled=True)  55.3 us
    all_gather x1, waiting for transfers between devices, shards(): lax.all_gather(occupied, 'row', axis=0, tiled=True)  45.5 us
    all_gather x1, waiting for transfers between devices, shards(): lax.all_gather(virtual, 'row', axis=0, tiled=True)  35.7 us
    all_to_all x1, blocking collectives, shards(): lax.all_to_all(shaped, 'col', split_axis=2, concat_axis=4, tiled=True)  35.4 us
    all_to_all x1, waiting for transfers between devices, shards(): lax.all_to_all(lax.all_to_all(layered, 'row', split_axis=1, concat_axis=0...  27.9 us
    psum x1, blocking collectives, shards(): lax.psum(lax.psum(partial_chi, axis_name='col'), axis_name='row')  27.7 us
  transfers between devices with their start and end apart: 4, of which 3 were waited for; matrix products, arithmetic and copies ran while one was open for 8% of the time, Pallas kernels for 0%

profile of v1, /device:TPU:0, one launch (start us, length us, event | category | flops | bytes accessed | tf_op | source)
XLA Modules:
  0.0 454.6 jit_solution(13387646627564546708)
XLA Ops:
  6.5 0.0 all-gather.3.cloned.1.call-start
  6.5 0.7 all-gather.3.cloned.1.call-update
  7.3 0.0 all-gather.5.cloned.1.call-start
  7.3 0.7 all-gather.5.cloned.1.call-update
  8.0 0.9 fusion.13
  8.9 0.1 broadcast_bitcast_fusion
  9.0 2.8 copy_multiply_fusion
  11.7 0.8 copy.15
  12.6 80.1 %all_to_all.66 = bf16[32,256,128]{2,1,0:T(8,128)(2,1)} all-to-all(bf16[32,256,128]{2,1,0:T(8,128)(2,1)S(1)} %copy.15), channel_id=1, replica_groups=mesh['aux'=2,'row'=8,'col'=16] {'row'}, dimensions={0} | all-to-all | bytes 4194304 | tf_op jit(solution)/shard_map/all_to_all | solution.py:33
  92.7 4.5 copy.16
  97.2 4.2 all_to_all.51
  101.4 45.5 %all-gather.3.cloned.1.call-done = bf16[2048,2048]{1,0:T(8,128)(2,1)} async-done(((bf16[256,2048]{1,0:T(8,128)(2,1)}), bf16[2048,2048]{1,0:T(8,128)(2,1)}) %all-gather.3.cloned.1.call-update) | async-done | bytes 8388624 | tf_op jit(solution)/shard_map/all_gather | solution.py:36
  146.9 9.8 %fusion.10 = bf16[4,2048,128]{1,2,0:T(8,128)(2,1)} fusion(bf16[4,2048,128]{1,2,0:T(8,128)(2,1)} %all_to_all.51, bf16[2048,2048]{1,0:T(8,128)(2,1)} %all-gather.3.cloned.1.call-done), kind=kOutput, calls=%fused_computation.6 | convolution fusion | flops 4296015872 | bytes 12582912 | tf_op jit(solution)/shard_map/ml,pmn->pln/dot_general | solution.py:39
  156.7 3.9 copy.17
  160.6 2.2 copy.18
  162.8 35.4 %all_to_all.67 = bf16[4,8,16,16,128]{4,3,1,0,2:T(8,128)(2,1)S(1)} all-to-all(bf16[4,8,16,16,128]{4,3,1,0,2:T(8,128)(2,1)S(1)} %copy.18), channel_id=1, replica_groups=mesh['aux'=2,'row'=8,'col'=16] {'col'}, dimensions={2} | all-to-all | bytes 4194304 | tf_op jit(solution)/shard_map/all_to_all | solution.py:44
  198.2 3.7 copy.19
  202.0 4.2 reshape.35
  206.2 35.7 %all-gather.5.cloned.1.call-done = bf16[2048,2048]{1,0:T(8,128)(2,1)} async-done(((bf16[256,2048]{1,0:T(8,128)(2,1)}), bf16[2048,2048]{1,0:T(8,128)(2,1)}) %all-gather.5.cloned.1.call-update) | async-done | bytes 8388624 | tf_op jit(solution)/shard_map/all_gather | solution.py:37
  241.9 8.5 %fusion.7 = bf16[4,128,2048]{2,1,0:T(8,128)(2,1)S(1)} fusion(bf16[4,128,2048]{2,1,0:T(8,128)(2,1)} %reshape.35, bf16[2048,2048]{1,0:T(8,128)(2,1)} %all-gather.5.cloned.1.call-done), kind=kOutput, calls=%fused_computation.5 | convolution fusion | flops 4296015872 | bytes 12582912 | tf_op jit(solution)/shard_map/pln,ns->pls/dot_general | solution.py:46
  250.4 0.6 copy.23
  251.0 0.6 copy.20
  251.6 55.3 %all_to_all.68 = bf16[4,8,1,16,16,128]{5,4,3,0,2,1:T(8,128)(2,1)S(1)} all-to-all(bf16[4,8,1,16,16,128]{5,4,3,0,2,1:T(8,128)(2,1)S(1)} %copy.20), channel_id=1, replica_groups=mesh['aux'=2,'row'=8,'col'=16] {'row'}, dimensions={1} | all-to-all | bytes 4194304 | tf_op jit(solution)/shard_map/all_to_all | solution.py:51
  306.9 1.8 copy.21
  308.8 6.9 %all-to-all-start.3 = ((bf16[32,1,1,16,16,128]{5,3,0,2,1,4:T(8,128)(2,1)}), bf16[32,1,1,16,16,128]{5,3,0,2,1,4:T(8,128)(2,1)}, u32[]{:S(2)}, u32[]{:S(2)}) async-start(bf16[32,1,1,16,16,128]{5,3,0,2,1,4:T(8,128)(2,1)} %copy.21), calls=%async_computation.3 | async-start | bytes 4194304 | tf_op jit(solution)/shard_map/all_to_all | solution.py:50
  315.6 0.1 collective-permute-start
  315.7 27.9 %all-to-all-done.3 = bf16[32,1,1,16,16,128]{5,3,0,2,1,4:T(8,128)(2,1)} async-done(((bf16[32,1,1,16,16,128]{5,3,0,2,1,4:T(8,128)(2,1)}), bf16[32,1,1,16,16,128]{5,3,0,2,1,4:T(8,128)(2,1)}, u32[]{:S(2)}, u32[]{:S(2)}) %all-to-all-start.3) | async-done | bytes 2097184 | tf_op jit(solution)/shard_map/all_to_all | solution.py:50
  343.7 2.1 copy.22
  345.8 0.7 convolution_bitcast_fusion.1
  346.5 0.0 collective-permute-done
  346.5 2.3 broadcast_select_fusion.1
  348.8 0.1 pad_maximum_fusion
  348.9 70.5 %psum.14 = f32[32,64]{1,0:T(8,128)S(1)} all-reduce(f32[32,64]{1,0:T(8,128)S(1)} %pad_maximum_fusion), channel_id=1, replica_groups=mesh['aux'=2,'row'=8,'col'=16] {'col'}, use_global_device_ids=true, to_apply=%region_0.1 | all-reduce | flops 2048 | bytes 16384 | tf_op jit(solution)/shard_map/psum | solution.py:64
  419.4 27.7 %psum.15 = f32[32,64]{1,0:T(8,128)S(1)} all-reduce(f32[32,64]{1,0:T(8,128)S(1)} %psum.14), channel_id=1, replica_groups=mesh['aux'=2,'row'=8,'col'=16] {'row'}, use_global_device_ids=true, to_apply=%region_1.2 | all-reduce | flops 2048 | bytes 16384 | tf_op jit(solution)/shard_map/psum | solution.py:64
  447.1 0.6 broadcast_multiply_fusion
Async XLA Ops:
  6.5 140.3 %all-gather.3.cloned.1.call-start = ((), (), s32[]{:S(2)}) async-start(), calls=%async_computation.4 | async-start | bytes 9437184 | tf_op jit(solution)/shard_map/all_gather | solution.py:36
  7.3 234.6 %all-gather.5.cloned.1.call-start = ((), (), s32[]{:S(2)}) async-start(), calls=%async_computation.5 | async-start | bytes 9437184 | tf_op jit(solution)/shard_map/all_gather | solution.py:37
  308.8 34.9 %all-to-all-start.3 = ((bf16[32,1,1,16,16,128]{5,3,0,2,1,4:T(8,128)(2,1)}), bf16[32,1,1,16,16,128]{5,3,0,2,1,4:T(8,128)(2,1)}, u32[]{:S(2)}, u32[]{:S(2)}) async-start(bf16[32,1,1,16,16,128]{5,3,0,2,1,4:T(8,128)(2,1)} %copy.21), calls=%async_computation.3 | async-start | bytes 4194304 | tf_op jit(solution)/shard_map/all_to_all | solution.py:50
  315.6 30.8 %collective-permute-start = (bf16[32,256,128]{2,0,1:T(8,128)(2,1)S(1)}, bf16[32,256,128]{2,0,1:T(8,128)(2,1)}, u32[]{:S(2)}, u32[]{:S(2)}) collective-permute-start(bf16[32,256,128]{2,0,1:T(8,128)(2,1)S(1)} %copy_multiply_fusion), channel_id=1, source_target_pairs={{0,128},{128,0},{1,129},{129,1},{2,130},{130,2},{3,131},{131,3},{4... | collective-permute-start | bytes 6291464 | tf_op jit(solution)/shard_map/ppermute | solution.py:13
Sparse Core Ops, SparseCore 0:
  9.1 137.6 all-gather.2
  148.7 93.1 all-gather.4

commit v2 on v0

--- a/solution.py
+++ b/solution.py
@@ -1,3 +1,4 @@
+import functools
 import jax
 import jax.numpy as jnp
 from jax import lax
@@ -5,6 +6,13 @@
 
 NAO = 2048
 TILE = 128
+
+
+def rounds_draft(z_in, mesh_ax):
+    return jnp.sum(lax.all_gather(z_in, mesh_ax), axis=0)
+
+
+treat_column = functools.partial(rounds_draft, mesh_ax=("row", "col"))
 
 
 def swapped(value, axis, apart):
@@ -61,7 +69,7 @@
     first_half = jnp.where(aux_idx == 0, with_mine, with_theirs)
     second_half = jnp.where(aux_idx == 0, with_theirs, with_mine)
     partial_chi = jnp.concatenate([first_half, second_half], axis=1)
-    total_chi = lax.psum(partial_chi, ("row", "col"))
+    total_chi = treat_column(partial_chi)
     return total_chi / NAO
 
 

time: 1040 us -> 470 us (0.45)
  blocking collectives: 853 us -> 171 us
  waiting for transfers between devices: 111 us -> 219 us
    psum x1 -> x0, blocking collectives: 682 us -> none  [shards(): total_chi = lax.psum(partial_chi, ('row', 'col'))]
    all_gather x0 -> x1, waiting for transfers between devices: none -> 109 us  [rounds_draft(): return jnp.sum(lax.all_gather(z_in, mesh_ax), axis=0)]
  transfers between devices with their start and end apart: 4 -> 5, of which waited for: 3 -> 4; matrix products, arithmetic and copies ran while one was open for 3% -> 8% of each run, Pallas kernels for 0% -> 0%
where the time goes in v2:
time: 470 us; the launch traced here: 467 us
  waiting for transfers between devices  219 us (47%)
  blocking collectives  171 us (36%)
  local copies, waits for them, and re-layouts  28.9 us (6%)
  matrix products  21.3 us (5%)
  between operations  13.2 us (3%)
  starting transfers between devices  7.03 us (1%)
  other arithmetic  6.74 us (1%)
    all_gather x1, waiting for transfers between devices, rounds_draft(): return jnp.sum(lax.all_gather(z_in, mesh_ax), axis=0)  109 us
    all_to_all x1, blocking collectives, shards(): lax.all_to_all(screened, 'row', split_axis=0, concat_axis=1, tiled=True)  80.1 us
    all_to_all x1, blocking collectives, shards(): lax.all_to_all(layered, 'row', split_axis=1, concat_axis=0, tiled=True)  55.3 us
    all_gather x1, waiting for transfers between devices, shards(): lax.all_gather(occupied, 'row', axis=0, tiled=True)  45.5 us
    all_gather x1, waiting for transfers between devices, shards(): lax.all_gather(virtual, 'row', axis=0, tiled=True)  35.7 us
    all_to_all x1, blocking collectives, shards(): lax.all_to_all(shaped, 'col', split_axis=2, concat_axis=4, tiled=True)  35.4 us
    all_to_all x1, waiting for transfers between devices, shards(): lax.all_to_all(lax.all_to_all(layered, 'row', split_axis=1, concat_axis=0...  27.9 us
    dot_general x1, matrix products, shards(): jnp.einsum('ml,pmn->pln', occ_all, moved, preferred_element_type=jnp.floa...  9.82 us
  transfers between devices with their start and end apart: 5, of which 4 were waited for; matrix products, arithmetic and copies ran while one was open for 8% of the time, Pallas kernels for 0%

profile of v2, /device:TPU:0, one launch (start us, length us, event | category | flops | bytes accessed | tf_op | source)
XLA Modules:
  0.0 467.1 jit_solution(16406083937011497203)
XLA Ops:
  6.5 0.0 all-gather.5.cloned.1.call-start
  6.5 0.7 all-gather.5.cloned.1.call-update
  7.3 0.0 all-gather.7.cloned.1.call-start
  7.3 0.7 all-gather.7.cloned.1.call-update
  8.0 0.9 fusion.13
  8.9 0.1 broadcast_bitcast_fusion
  9.0 2.8 copy_multiply_fusion
  11.7 0.8 copy.15
  12.6 80.1 %all_to_all.66 = bf16[32,256,128]{2,1,0:T(8,128)(2,1)} all-to-all(bf16[32,256,128]{2,1,0:T(8,128)(2,1)S(1)} %copy.15), channel_id=1, replica_groups=mesh['aux'=2,'row'=8,'col'=16] {'row'}, dimensions={0} | all-to-all | bytes 4194304 | tf_op jit(solution)/shard_map/all_to_all | solution.py:41
  92.7 4.5 copy.16
  97.2 4.2 all_to_all.51
  101.4 45.5 %all-gather.5.cloned.1.call-done = bf16[2048,2048]{1,0:T(8,128)(2,1)} async-done(((bf16[256,2048]{1,0:T(8,128)(2,1)}), bf16[2048,2048]{1,0:T(8,128)(2,1)}) %all-gather.5.cloned.1.call-update) | async-done | bytes 8388624 | tf_op jit(solution)/shard_map/all_gather | solution.py:44
  146.9 9.8 %fusion.10 = bf16[4,2048,128]{1,2,0:T(8,128)(2,1)} fusion(bf16[4,2048,128]{1,2,0:T(8,128)(2,1)} %all_to_all.51, bf16[2048,2048]{1,0:T(8,128)(2,1)} %all-gather.5.cloned.1.call-done), kind=kOutput, calls=%fused_computation.6 | convolution fusion | flops 4296015872 | bytes 12582912 | tf_op jit(solution)/shard_map/ml,pmn->pln/dot_general | solution.py:47
  156.7 4.0 copy.17
  160.6 2.2 copy.18
  162.8 35.4 %all_to_all.67 = bf16[4,8,16,16,128]{4,3,1,0,2:T(8,128)(2,1)S(1)} all-to-all(bf16[4,8,16,16,128]{4,3,1,0,2:T(8,128)(2,1)S(1)} %copy.18), channel_id=1, replica_groups=mesh['aux'=2,'row'=8,'col'=16] {'col'}, dimensions={2} | all-to-all | bytes 4194304 | tf_op jit(solution)/shard_map/all_to_all | solution.py:52
  198.3 3.8 copy.19
  202.0 4.2 reshape.35
  206.2 35.7 %all-gather.7.cloned.1.call-done = bf16[2048,2048]{1,0:T(8,128)(2,1)} async-done(((bf16[256,2048]{1,0:T(8,128)(2,1)}), bf16[2048,2048]{1,0:T(8,128)(2,1)}) %all-gather.7.cloned.1.call-update) | async-done | bytes 8388624 | tf_op jit(solution)/shard_map/all_gather | solution.py:45
  241.9 8.5 %fusion.7 = bf16[4,128,2048]{2,1,0:T(8,128)(2,1)S(1)} fusion(bf16[4,128,2048]{2,1,0:T(8,128)(2,1)} %reshape.35, bf16[2048,2048]{1,0:T(8,128)(2,1)} %all-gather.7.cloned.1.call-done), kind=kOutput, calls=%fused_computation.5 | convolution fusion | flops 4296015872 | bytes 12582912 | tf_op jit(solution)/shard_map/pln,ns->pls/dot_general | solution.py:54
  250.4 0.6 copy.23
  251.0 0.6 copy.20
  251.6 55.3 %all_to_all.68 = bf16[4,8,1,16,16,128]{5,4,3,0,2,1:T(8,128)(2,1)S(1)} all-to-all(bf16[4,8,1,16,16,128]{5,4,3,0,2,1:T(8,128)(2,1)S(1)} %copy.20), channel_id=1, replica_groups=mesh['aux'=2,'row'=8,'col'=16] {'row'}, dimensions={1} | all-to-all | bytes 4194304 | tf_op jit(solution)/shard_map/all_to_all | solution.py:59
  306.9 1.9 copy.21
  308.8 6.9 %all-to-all-start.3 = ((bf16[32,1,1,16,16,128]{5,3,0,2,1,4:T(8,128)(2,1)}), bf16[32,1,1,16,16,128]{5,3,0,2,1,4:T(8,128)(2,1)}, u32[]{:S(2)}, u32[]{:S(2)}) async-start(bf16[32,1,1,16,16,128]{5,3,0,2,1,4:T(8,128)(2,1)} %copy.21), calls=%async_computation.3 | async-start | bytes 4194304 | tf_op jit(solution)/shard_map/all_to_all | solution.py:58
  315.6 0.0 all-gather.9.cloned.1.call-start
  315.7 0.1 collective-permute-start
  315.8 27.9 %all-to-all-done.3 = bf16[32,1,1,16,16,128]{5,3,0,2,1,4:T(8,128)(2,1)} async-done(((bf16[32,1,1,16,16,128]{5,3,0,2,1,4:T(8,128)(2,1)}), bf16[32,1,1,16,16,128]{5,3,0,2,1,4:T(8,128)(2,1)}, u32[]{:S(2)}, u32[]{:S(2)}) %all-to-all-start.3) | async-done | bytes 2097184 | tf_op jit(solution)/shard_map/all_to_all | solution.py:58
  343.7 2.1 copy.22
  345.8 0.7 convolution_bitcast_fusion.1
  346.5 0.0 collective-permute-done
  346.5 2.3 broadcast_select_fusion.1
  348.8 0.7 pad_maximum_fusion
  349.5 0.0 all-gather.9.cloned.1.call-update
  349.5 108.7 %all-gather.9.cloned.1.call-done = f32[4096,64]{1,0:T(8,128)} async-done(((f32[32,64]{1,0:T(8,128)}), f32[4096,64]{1,0:T(8,128)}) %all-gather.9.cloned.1.call-update) | async-done | bytes 1048592 | tf_op jit(solution)/shard_map/all_gather | solution.py:12
  458.2 1.8 reduce_sum.9
  460.0 0.6 broadcast_multiply_fusion
Async XLA Ops:
  6.5 140.3 %all-gather.5.cloned.1.call-start = ((), (), s32[]{:S(2)}) async-start(), calls=%async_computation.4 | async-start | bytes 9437184 | tf_op jit(solution)/shard_map/all_gather | solution.py:44
  7.3 234.6 %all-gather.7.cloned.1.call-start = ((), (), s32[]{:S(2)}) async-start(), calls=%async_computation.5 | async-start | bytes 9437184 | tf_op jit(solution)/shard_map/all_gather | solution.py:45
  308.8 34.9 %all-to-all-start.3 = ((bf16[32,1,1,16,16,128]{5,3,0,2,1,4:T(8,128)(2,1)}), bf16[32,1,1,16,16,128]{5,3,0,2,1,4:T(8,128)(2,1)}, u32[]{:S(2)}, u32[]{:S(2)}) async-start(bf16[32,1,1,16,16,128]{5,3,0,2,1,4:T(8,128)(2,1)} %copy.21), calls=%async_computation.3 | async-start | bytes 4194304 | tf_op jit(solution)/shard_map/all_to_all | solution.py:58
  315.6 142.5 %all-gather.9.cloned.1.call-start = ((), (), s32[]{:S(2)}) async-start(), calls=%async_computation.6 | async-start | bytes 2113536 | tf_op jit(solution)/shard_map/all_gather | solution.py:12
  315.7 30.8 %collective-permute-start = (bf16[32,256,128]{2,0,1:T(8,128)(2,1)S(1)}, bf16[32,256,128]{2,0,1:T(8,128)(2,1)}, u32[]{:S(2)}, u32[]{:S(2)}) collective-permute-start(bf16[32,256,128]{2,0,1:T(8,128)(2,1)S(1)} %copy_multiply_fusion), channel_id=1, source_target_pairs={{0,128},{128,0},{1,129},{129,1},{2,130},{130,2},{3,131},{131,3},{4... | collective-permute-start | bytes 6291464 | tf_op jit(solution)/shard_map/ppermute | solution.py:21
Sparse Core Ops, SparseCore 0:
  9.1 137.6 all-gather.4
  148.7 93.1 all-gather.6
  349.6 108.4 all-gather.8
